TPU v7x, 256 devices: a whole 4x4x8 slice. The times are simulated.
256 devices in a mesh: replica: 64 (over x, z, core), shard: 4 (over y).
Axes of the slice: x: 4, y: 4, z: 8, core: 2. Of those that a mesh axis runs over, the one named last changes fastest.
Arguments:
- activations: bfloat16 [65536, 1536], P('replica'), may hold values from -6 to 6
- output_grads: bfloat16 [65536, 4, 1536], P('replica', None, 'shard'), may hold values from -0.00390625 to 0.00390625
- owner: int32 [4], replicated, may hold values from 0 to 3, each once
- step_count: int32 [1], replicated, may hold values from 1 to 40
- statistics: float32 [6144, 2, 1536], P(('replica', 'shard')), may hold values from -6 to 6
- inverse_roots: bfloat16 [6144, 2, 1536], P(('replica', 'shard')), may hold values from -1 to 2, as said below
- first_moment: float32 [6144, 1536], P(('replica', 'shard')), may hold values from -0.6 to 0.6
- second_moment: float32 [6144, 1536], P(('replica', 'shard')), may hold values from 0.005 to 0.05
Outputs:
- new_statistics: float32 [6144, 2, 1536], P(('replica', 'shard'))
- new_first: float32 [6144, 1536], P(('replica', 'shard'))
- new_second: float32 [6144, 1536], P(('replica', 'shard'))
- update: bfloat16 [4, 1536, 1536], P(None, None, 'shard')
Inputs may be any that keep to these rules, and one draw needn't show every extreme that they name: A permutation: block b belongs to the group of replicas b' * (16) to (b' + 1) * 16 - 1 with b' = owner[b]. `inverse_roots`: each matrix has positive diagonal entries.
All inputs are finite; a program needn't handle non-finite values.
Results may differ from a plain program's by a relative error of at most 0.0049.
Values may be sent and summed in bfloat16 or wider, within the bound.
No kernel may reach another device: no remote copies, remote signals or barrier semaphores. Data moves between devices by JAX's collectives and lax.ppermute only.
A program may use at most 128 MiB of HBM per device.

v0:
```python
import functools
import math

import jax
import jax.numpy as jnp
from jax import lax
from jax.sharding import Mesh
from jax.sharding import PartitionSpec as P

REPLICA = ("replica_0", "replica_1", "replica_2")
REPLICA_SHARD = ("replica_0", "replica_1", "replica_2", "shard")


beta_stat = 0.9
beta_first = 0.9
beta_second = 0.999
eps_adam = 1e-08
eps_norm = 1e-06


def in_order(pieces, dim):
    shape = list(pieces.shape[1:])
    shape[dim] *= pieces.shape[0]
    return jnp.moveaxis(pieces, 0, dim).reshape(shape)


def copy_for_each(value, axis):
    copies = jnp.broadcast_to(value, (lax.axis_size(axis), *value.shape))
    return lax.all_to_all(copies, axis, split_axis=0, concat_axis=0, tiled=True)


def gather_directly(value, axis, dim):
    return in_order(copy_for_each(value, axis), dim)


def partner_2(value, axis, apart):
    return lax.ppermute(value, axis, [(i, i ^ 1 << apart) for i in range(lax.axis_size(axis))])


def reduced_to_own(pieces, axes, order):
    shape = [lax.axis_size(a) for a in axes]
    pieces = pieces.reshape(*shape, *pieces.shape[1:])
    pieces = pieces.transpose(*order, *range(len(axes), pieces.ndim))
    pieces = pieces.reshape(-1, *pieces.shape[len(axes) :])
    for k in order:
        pieces = lax.psum_scatter(pieces, axes[k], scatter_dimension=0, tiled=True)
    return pieces[0]


def cut_along(value, dim, length):
    before, after = (value.shape[:dim], value.shape[dim + 1 :])
    return jnp.moveaxis(value.reshape(*before, length, -1, *after), dim, 0)


def scatter_axes(value, axes, order, dim):
    length = lax.axis_size(axes)
    return reduced_to_own(cut_along(value, dim, length), axes, order)


def one_axis_at_a_time(value, axes):
    return functools.reduce(lax.psum, axes, value)


def butterfly(values, concat_axis, group_bits, swap_values):
    position = lax.axis_index(REPLICA)
    for bit_number in range(group_bits):
        partner = swap_values(values, bit_number)
        upper = position >> bit_number & 1 == 1
        values = jnp.where(
            upper,
            jnp.concatenate([partner, values], concat_axis),
            jnp.concatenate([values, partner], concat_axis),
        )
    return values


def body(
    activations,
    output_grads,
    owner,
    step_count,
    statistics,
    inverse_roots,
    first_moment,
    second_moment,
):
    model_width = activations.shape[1]
    blocks_count = output_grads.shape[1]
    replicas = lax.axis_size(REPLICA)
    shards = lax.axis_size("shard")
    group_size = replicas // blocks_count
    group_bits = group_size.bit_length() - 1
    rows_dev = blocks_count * model_width // replicas
    span_rows = statistics.shape[0]
    owner_slot = lax.axis_index(REPLICA) // group_size
    local_index = lax.axis_index(REPLICA) % group_size
    span_index = local_index * shards + lax.axis_index("shard")
    root_rows = gather_directly(inverse_roots[:, 1, :], "shard", 0)
    whole_root = butterfly(
        root_rows, 0, group_bits, lambda values, bit_number: partner_2(values, REPLICA, bit_number)
    )
    slot_ids = jnp.arange(blocks_count, dtype=jnp.int32)
    onehot = (owner[None, :] == slot_ids[:, None]).astype(jnp.int32)
    source = jnp.sum(onehot * slot_ids[None, :], axis=1)
    grads_slot = jnp.take(output_grads, source, axis=1)
    piece_rows = math.gcd(rows_dev * lax.axis_size(REPLICA), model_width)

    def piece_product(piece_number):
        first_row = piece_number * piece_rows
        block_slot = first_row // model_width
        douts = lax.dynamic_index_in_dim(grads_slot, block_slot, 1, keepdims=False)
        return lax.dot_general(
            activations, douts, (((0,), (0,)), ((), ())), preferred_element_type=jnp.float32
        )

    pieces = lax.map(
        piece_product, jnp.arange(rows_dev * lax.axis_size(REPLICA) // piece_rows, dtype=jnp.int32)
    )
    reduced = scatter_axes(
        pieces.reshape(rows_dev * lax.axis_size(REPLICA), pieces.shape[-1]), REPLICA, (2, 0, 1), 0
    )
    exact_rows = lax.all_to_all(
        reduced.astype(jnp.bfloat16), "shard", split_axis=0, concat_axis=1, tiled=True
    ).astype(reduced.dtype)
    rounded = exact_rows.astype(jnp.bfloat16)
    block_rows = gather_directly(rounded, "shard", 0)
    full_grad = butterfly(
        block_rows, 0, group_bits, lambda values, bit_number: partner_2(values, REPLICA, bit_number)
    )
    grad_columns = lax.dynamic_slice_in_dim(full_grad, span_index * span_rows, span_rows, 1)
    left_gram = lax.dot_general(
        rounded, full_grad, (((1,), (1,)), ((), ())), preferred_element_type=jnp.float32
    )
    right_gram = lax.dot_general(
        grad_columns, full_grad, (((0,), (0,)), ((), ())), preferred_element_type=jnp.float32
    )
    new_left = beta_stat * statistics[:, 0, :] + (1.0 - beta_stat) * left_gram
    new_right = beta_stat * statistics[:, 1, :] + (1.0 - beta_stat) * right_gram
    count_float = step_count[0].astype(jnp.float32)
    first_new = beta_first * first_moment + (1.0 - beta_first) * exact_rows
    second_new = beta_second * second_moment + (1.0 - beta_second) * exact_rows * exact_rows
    first_hat = first_new / (1.0 - jnp.power(beta_first, count_float))
    second_hat = second_new / (1.0 - jnp.power(beta_second, count_float))
    adam_dir = first_hat / (jnp.sqrt(second_hat) + eps_adam)
    left_root = inverse_roots[:, 0, :]
    left_part = jnp.dot(left_root, full_grad, preferred_element_type=jnp.float32)
    precond = lax.dot_general(
        left_part,
        whole_root.astype(jnp.float32),
        (((1,), (1,)), ((), ())),
        precision=lax.Precision.HIGHEST,
    )
    slot_mask = (slot_ids == owner_slot).astype(jnp.float32)
    adam_total, precond_total = (
        one_axis_at_a_time(slot_mask * jnp.sum(adam_dir * adam_dir), REPLICA_SHARD),
        one_axis_at_a_time(slot_mask * jnp.sum(precond * precond), REPLICA_SHARD),
    )
    adam_squares = jnp.sum(adam_total * slot_mask)
    precond_squares = jnp.sum(precond_total * slot_mask)
    scale = jnp.sqrt(adam_squares) / (jnp.sqrt(precond_squares) + eps_norm)
    grafted = (precond * scale).astype(jnp.bfloat16)
    feature_rows = lax.all_to_all(grafted, "shard", split_axis=1, concat_axis=0, tiled=True)
    every_block = lax.all_gather(feature_rows, REPLICA, axis=0, tiled=True)
    update = jnp.take(
        every_block.reshape(blocks_count, model_width, every_block.shape[-1]), owner, axis=0
    )
    new_stats = jnp.stack([new_left, new_right], axis=1)
    return (new_stats, first_new, second_new, update)


def solution(mesh):
    torus = Mesh(
        mesh.devices.reshape(4, 8, 2, mesh.shape["shard"]),
        ("replica_0", "replica_1", "replica_2", "shard"),
    )
    placed = (
        P(REPLICA, None),
        P(REPLICA, None, "shard"),
        P(),
        P(),
        P(REPLICA_SHARD, None, None),
        P(REPLICA_SHARD, None, None),
        P(REPLICA_SHARD, None),
        P(REPLICA_SHARD, None),
    )
    return jax.shard_map(
        body,
        mesh=torus,
        in_specs=placed,
        out_specs=(
            P(REPLICA_SHARD, None, None),
            P(REPLICA_SHARD, None),
            P(REPLICA_SHARD, None),
            P(None, None, "shard"),
        ),
        check_vma=False,
    )
```

profile of v0, /device:TPU:1, one launch (start us, length us, event | category | flops | bytes accessed | tf_op | source)
XLA Modules:
  0.0 700.0 jit_solution(6775838303506029115)
XLA Ops:
  9.1 16.4 %gather_fusion = bf16[4,1024,384]{2,0,1:T(4,128)(2,1)} fusion(bf16[1024,4,384]{2,1,0:T(4,128)(2,1)S(1)} %copy-done, s32[1024]{0:T(1024)S(1)} %pad_clamp_fusion.1), kind=kCustom, calls=%fused_computation | custom fusion | bytes 6291472 | tf_op jit(solution)/shard_map/jit(_take)/gather | solution.py:105
  25.5 3.3 select_bitcast_fusion
  30.9 39.4 %while.12 = (s32[]{:T(128)}, f32[4,1536,384]{2,1,0:T(8,128)}, s32[4]{0:T(128)S(1)}, bf16[1024,4,384]{2,0,1:T(8,128)(2,1)}, bf16[1024,1536]{1,0:T(8,128)(2,1)}, /...) while((s32[]{:T(128)}, f32[4,1536,384]{2,1,0:T(8,128)}, ...), condition=%wide.region_2.3_spmd, body=%wide.region_1.2_spmd.sunk | while | flops 1207959552 | bytes 15728909 | solution.py:116
  32.1 5.0 convolution_bitcast_fusion.2
  41.9 5.0 convolution_bitcast_fusion.2
  51.9 5.0 convolution_bitcast_fusion.2
  61.7 5.0 convolution_bitcast_fusion.2
  70.3 8.1 %copy.28 = f32[2,4,8,96,384]{4,3,2,1,0:T(8,128)} copy(f32[2,4,8,96,384]{4,3,0,2,1:T(8,128)} %bitcast.70) | data formatting | bytes 18874368 | tf_op jit(solution)/shard_map/transpose | solution.py:43
  78.5 27.6 %reduce-scatter.4.cloned.1.call-done = f32[32,96,384]{2,1,0:T(8,128)} async-done(((f32[64,96,384]{2,1,0:T(8,128)}), f32[32,96,384]{2,1,0:T(8,128)}) %reduce-scatter.4.cloned.1.call-update) | async-done | bytes 4718608 | tf_op jit(solution)/shard_map/reduce_scatter | solution.py:46
  106.1 57.0 %reduce-scatter.6.cloned.1.call-done = f32[8,96,384]{2,1,0:T(8,128)} async-done(((f32[32,96,384]{2,1,0:T(8,128)}), f32[8,96,384]{2,1,0:T(8,128)}) %reduce-scatter.6.cloned.1.call-update) | async-done | bytes 1179664 | tf_op jit(solution)/shard_map/reduce_scatter | solution.py:46
  163.2 36.9 %reduce-scatter.8.cloned.1.call-done = f32[1,96,384]{2,1,0:T(8,128)} async-done(((f32[8,96,384]{2,1,0:T(8,128)}), f32[1,96,384]{2,1,0:T(8,128)}) %reduce-scatter.8.cloned.1.call-update) | async-done | bytes 147472 | tf_op jit(solution)/shard_map/reduce_scatter | solution.py:46
  201.0 8.1 %all_to_all.45 = bf16[4,24,384]{2,1,0:T(8,128)(2,1)S(1)} all-to-all(bf16[4,24,384]{2,1,0:T(8,128)(2,1)S(1)} %bitcast.80), channel_id=1, replica_groups=mesh['replica_0'=4,'replica_1'=8,'replica_2'=2,'shard'=4] {'shard'}, dimensions={0} | all-to-all | bytes 147456 | tf_op jit(solution)/shard_map/all_to_all | solution.py:122
  209.2 8.1 %all_to_all.46 = bf16[4,24,1536]{2,1,0:T(8,128)(2,1)S(1)} all-to-all(bf16[4,24,1536]{2,1,0:T(8,128)(2,1)S(1)} %broadcast_in_dim.44), channel_id=1, replica_groups=mesh['replica_0'=4,'replica_1'=8,'replica_2'=2,'shard'=4] {'shard'}, dimensions={0} | all-to-all | bytes 589824 | tf_op jit(solution)/shard_map/all_to_all | solution.py:29
  217.2 7.8 %collective-permute-start = (bf16[96,1536]{1,0:T(8,128)(2,1)S(1)}, bf16[96,1536]{1,0:T(8,128)(2,1)S(1)}, u32[]{:S(2)}, u32[]{:S(2)}) collective-permute-start(bf16[96,1536]{1,0:T(8,128)(2,1)S(1)} %bitcast.72), channel_id=1, source_target_pairs={{0,4},{4,0},{8,12},{12,8},{16,20},{20,16},{24,28},{28,24},{32,36},... | collective-permute-start | bytes 884744 | tf_op jit(solution)/shard_map/ppermute | solution.py:37
  228.1 3.5 all-to-all-start.2
  231.6 6.1 all-to-all-done.2
  244.8 35.8 %collective-permute-done.5 = bf16[192,1536]{1,0:T(8,128)(2,1)S(1)} collective-permute-done((bf16[192,1536]{1,0:T(8,128)(2,1)S(1)}, bf16[192,1536]{1,0:T(8,128)(2,1)S(1)}, u32[]{:S(2)}, u32[]{:S(2)}) %collective-permute-start.5) | collective-permute-done | bytes 589856 | tf_op jit(solution)/shard_map/ppermute | solution.py:37
  282.9 37.5 %collective-permute-done.2 = bf16[384,1536]{1,0:T(8,128)(2,1)} collective-permute-done((bf16[384,1536]{1,0:T(8,128)(2,1)S(1)}, bf16[384,1536]{1,0:T(8,128)(2,1)}, u32[]{:S(2)}, u32[]{:S(2)}) %collective-permute-start.2) | collective-permute-done | bytes 1179680 | tf_op jit(solution)/shard_map/ppermute | solution.py:37
  320.4 2.7 maximum_select_fusion.3
  325.6 71.3 %collective-permute-done.6 = bf16[384,1536]{1,0:T(8,128)(2,1)S(1)} collective-permute-done((bf16[384,1536]{1,0:T(8,128)(2,1)S(1)}, bf16[384,1536]{1,0:T(8,128)(2,1)S(1)}, u32[]{:S(2)}, u32[]{:S(2)}) %collective-permute-start.6) | collective-permute-done | bytes 1179680 | tf_op jit(solution)/shard_map/ppermute | solution.py:37
  403.8 4.0 maximum_select_fusion
  410.7 142.4 %collective-permute-done.7 = bf16[768,1536]{1,0:T(8,128)(2,1)} collective-permute-done((bf16[768,1536]{1,0:T(8,128)(2,1)}, bf16[768,1536]{1,0:T(8,128)(2,1)}, u32[]{:S(2)}, u32[]{:S(2)}) %collective-permute-start.7) | collective-permute-done | bytes 2359328 | tf_op jit(solution)/shard_map/ppermute | solution.py:37
  553.1 7.1 %multiply_reduce_fusion = (f32[]{:T(128)}, f32[24,1536]{1,0:T(8,128)S(1)}) fusion(f32[1536,24]{0,1:T(8,128)S(1)} %fusion.19, bf16[768,1536]{1,0:T(8,128)(2,1)} %maximum_select_fusion.4, bf16[768,1536]{1,0:T(8,128)(2,1)} %collective-permute-done.7, pred[]{:T(512)S(6)} %eq.40), kind=kOutput, calls=%fused_computation.41 | convolution fusion | flops 700784640 | bytes 5013509 | tf_op jit(solution)/shard_map/dot_general | solution.py:147
  560.8 8.3 %all-reduce.2 = (f32[4]{0:T(128)S(1)}, f32[4]{0:T(128)S(1)}) all-reduce(f32[4]{0:T(128)S(1)} %fusion.22, f32[4]{0:T(128)S(1)} %fusion.21), channel_id=1, replica_groups=mesh['replica_0'=4,'replica_1'=8,'replica_2'=2,'shard'=4] {'replica_0'}, use_global_device_ids=true, to_apply=%region_7.8 | all-reduce | flops 8 | bytes 64 | tf_op jit(solution)/shard_map/psum | solution.py:61
  569.1 11.1 %all-reduce = (f32[4]{0:T(128)S(1)}, f32[4]{0:T(128)S(1)}) all-reduce(f32[4]{0:T(128)S(1)} %get-tuple-element.107, f32[4]{0:T(128)S(1)} %get-tuple-element.108), channel_id=1, replica_groups=mesh['replica_0'=4,'replica_1'=8,'replica_2'=2,'shard'=4] {'replica_1'}, use_global_device_ids=true, to_apply=%region_8.9 | all-reduce | flops 8 | bytes 64 | tf_op jit(solution)/shard_map/psum | solution.py:61
  580.2 8.4 %all-reduce.3 = (f32[4]{0:T(128)S(1)}, f32[4]{0:T(128)S(1)}) all-reduce(f32[4]{0:T(128)S(1)} %get-tuple-element.103, f32[4]{0:T(128)S(1)} %get-tuple-element.104), channel_id=1, replica_groups=mesh['replica_0'=4,'replica_1'=8,'replica_2'=2,'shard'=4] {'replica_2'}, use_global_device_ids=true, to_apply=%region_9.10 | all-reduce | flops 8 | bytes 64 | tf_op jit(solution)/shard_map/psum | solution.py:61
  588.6 6.8 all-reduce.1
  597.6 7.6 %all_to_all.47 = bf16[24,4,384]{2,0,1:T(8,128)(2,1)} all-to-all(bf16[24,4,384]{2,0,1:T(8,128)(2,1)S(1)} %bitcast.84), channel_id=1, replica_groups=mesh['replica_0'=4,'replica_1'=8,'replica_2'=2,'shard'=4] {'shard'}, dimensions={1} | all-to-all | bytes 147456 | tf_op jit(solution)/shard_map/all_to_all | solution.py:162
  605.5 3.6 fusion.12
  611.5 70.9 %all-gather.2.cloned.1.call-done = bf16[6144,384]{1,0:T(8,128)(2,1)} async-done(((bf16[96,384]{1,0:T(8,128)(2,1)}), bf16[6144,384]{1,0:T(8,128)(2,1)}) %all-gather.2.cloned.1.call-update) | async-done | bytes 4718608 | tf_op jit(solution)/shard_map/all_gather | solution.py:163
  682.4 5.9 gather_fusion.1
  688.3 5.1 broadcast_select_fusion
  (83 shorter events, 49.9 us)
Async XLA Ops:
  7.2 1.9 copy-start
  7.2 98.9 %reduce-scatter.4.cloned.1.call-start = ((), (), s32[]{:S(2)}) async-start(), calls=%async_computation.7 | async-start | bytes 14155776 | tf_op jit(solution)/shard_map/reduce_scatter | solution.py:46
  78.4 84.7 %reduce-scatter.6.cloned.1.call-start = ((), (), s32[]{:S(2)}) async-start(), calls=%async_computation.8 | async-start | bytes 5898240 | tf_op jit(solution)/shard_map/reduce_scatter | solution.py:46
  106.0 121.1 %copy-start.5 = (bf16[24,2,1536]{2,1,0:T(2,128)(2,1)S(1)}, bf16[24,2,1536]{2,1,0:T(2,128)(2,1)}, u32[]{:S(2)}) copy-start(bf16[24,2,1536]{2,1,0:T(2,128)(2,1)} %param.15) | copy-start | bytes 442372
  106.1 94.0 %reduce-scatter.8.cloned.1.call-start = ((), (), s32[]{:S(2)}) async-start(), calls=%async_computation.9 | async-start | bytes 1327104 | tf_op jit(solution)/shard_map/reduce_scatter | solution.py:46
  217.2 9.0 %collective-permute-start = (bf16[96,1536]{1,0:T(8,128)(2,1)S(1)}, bf16[96,1536]{1,0:T(8,128)(2,1)S(1)}, u32[]{:S(2)}, u32[]{:S(2)}) collective-permute-start(bf16[96,1536]{1,0:T(8,128)(2,1)S(1)} %bitcast.72), channel_id=1, source_target_pairs={{0,4},{4,0},{8,12},{12,8},{16,20},{20,16},{24,28},{28,24},{32,36},... | collective-permute-start | bytes 884744 | tf_op jit(solution)/shard_map/ppermute | solution.py:37
  226.3 14.6 %collective-permute-start.1 = (bf16[192,1536]{1,0:T(8,128)(2,1)S(1)}, bf16[192,1536]{1,0:T(8,128)(2,1)S(1)}, u32[]{:S(2)}, u32[]{:S(2)}) collective-permute-start(bf16[192,1536]{1,0:T(8,128)(2,1)S(1)} %maximum_select_fusion.7), channel_id=1, source_target_pairs={{0,8},{4,12},{8,0},{12,4},{16,24},{20,28},{24,16},{28,20},{32,40},... | collective-permute-start | bytes 1769480 | tf_op jit(solution)/shard_map/ppermute | solution.py:37
  228.1 9.6 %all-to-all-start.2 = ((bf16[4,24,1536]{2,1,0:T(8,128)(2,1)}), bf16[4,24,1536]{2,1,0:T(8,128)(2,1)S(1)}, u32[]{:S(2)}, u32[]{:S(2)}) async-start(bf16[4,24,1536]{2,1,0:T(8,128)(2,1)} %broadcast_in_dim.46), calls=%async_computation.5 | async-start | bytes 589824 | tf_op jit(solution)/shard_map/all_to_all | solution.py:29
  231.5 450.9 %all-gather.2.cloned.1.call-start = ((), (), s32[]{:S(2)}) async-start(), calls=%async_computation.10 | async-start | bytes 4792320 | tf_op jit(solution)/shard_map/all_gather | solution.py:163
  237.7 5.8 collective-permute-start.4
  241.4 41.5 %copy-start.4 = (bf16[384,1536]{1,0:T(8,128)(2,1)}, bf16[384,1536]{1,0:T(8,128)(2,1)S(1)}, u32[]{:S(2)}) copy-start(bf16[384,1536]{1,0:T(8,128)(2,1)S(1)} %maximum_select_fusion.5) | copy-start | bytes 3538948
  241.4 79.0 %collective-permute-start.2 = (bf16[384,1536]{1,0:T(8,128)(2,1)S(1)}, bf16[384,1536]{1,0:T(8,128)(2,1)}, u32[]{:S(2)}, u32[]{:S(2)}) collective-permute-start(bf16[384,1536]{1,0:T(8,128)(2,1)S(1)} %maximum_select_fusion.5), channel_id=1, source_target_pairs={{0,16},{4,20},{8,24},{12,28},{16,0},{20,4},{24,8},{28,12},{32,48},... | collective-permute-start | bytes 3538952 | tf_op jit(solution)/shard_map/ppermute | solution.py:37
  243.6 37.0 %collective-permute-start.5 = (bf16[192,1536]{1,0:T(8,128)(2,1)S(1)}, bf16[192,1536]{1,0:T(8,128)(2,1)S(1)}, u32[]{:S(2)}, u32[]{:S(2)}) collective-permute-start(bf16[192,1536]{1,0:T(8,128)(2,1)S(1)} %maximum_select_fusion.8), channel_id=1, source_target_pairs={{0,8},{4,12},{8,0},{12,4},{16,24},{20,28},{24,16},{28,20},{32,40},... | collective-permute-start | bytes 1769480 | tf_op jit(solution)/shard_map/ppermute | solution.py:37
  280.9 115.9 %collective-permute-start.6 = (bf16[384,1536]{1,0:T(8,128)(2,1)S(1)}, bf16[384,1536]{1,0:T(8,128)(2,1)S(1)}, u32[]{:S(2)}, u32[]{:S(2)}) collective-permute-start(bf16[384,1536]{1,0:T(8,128)(2,1)S(1)} %maximum_select_fusion.6), channel_id=1, source_target_pairs={{0,16},{4,20},{8,24},{12,28},{16,0},{20,4},{24,8},{28,12},{32,48},... | collective-permute-start | bytes 3538952 | tf_op jit(solution)/shard_map/ppermute | solution.py:37
  323.1 78.6 %copy-start.7 = (f32[24,1536]{1,0:T(8,128)S(1)}, f32[24,1536]{1,0:T(8,128)}, u32[]{:S(2)}) copy-start(f32[24,1536]{1,0:T(8,128)} %param.17) | copy-start | bytes 442372
  323.1 78.6 %copy-start.8 = (f32[24,1536]{1,0:T(8,128)S(1)}, f32[24,1536]{1,0:T(8,128)}, u32[]{:S(2)}) copy-start(f32[24,1536]{1,0:T(8,128)} %param.16) | copy-start | bytes 442372
  323.1 80.8 %collective-permute-start.3 = (bf16[768,1536]{1,0:T(8,128)(2,1)S(1)}, bf16[768,1536]{1,0:T(8,128)(2,1)}, u32[]{:S(2)}, u32[]{:S(2)}) collective-permute-start(bf16[768,1536]{1,0:T(8,128)(2,1)S(1)} %maximum_select_fusion.3), channel_id=1, source_target_pairs={{0,32},{4,36},{8,40},{12,44},{16,48},{20,52},{24,56},{28,60},{32,0... | collective-permute-start | bytes 7077896 | tf_op jit(solution)/shard_map/ppermute | solution.py:37
  398.6 154.5 %collective-permute-start.7 = (bf16[768,1536]{1,0:T(8,128)(2,1)}, bf16[768,1536]{1,0:T(8,128)(2,1)}, u32[]{:S(2)}, u32[]{:S(2)}) collective-permute-start(bf16[768,1536]{1,0:T(8,128)(2,1)} %maximum_select_fusion.4), channel_id=1, source_target_pairs={{0,32},{4,36},{8,40},{12,44},{16,48},{20,52},{24,56},{28,60},{32,0... | collective-permute-start | bytes 7077896 | tf_op jit(solution)/shard_map/ppermute | solution.py:37
  407.8 2.2 copy-start.2
  410.7 194.5 %copy-start.9 = (s32[4]{0:T(128)S(1)}, s32[4]{0:T(128)}, u32[]{:S(2)}) copy-start(s32[4]{0:T(128)} %param.12) | copy-start | bytes 52
  410.7 194.5 %copy-start.6 = (f32[24,2,1536]{2,1,0:T(2,128)S(1)}, f32[24,2,1536]{2,1,0:T(2,128)}, u32[]{:S(2)}) copy-start(f32[24,2,1536]{2,1,0:T(2,128)} %param.14) | copy-start | bytes 884740
  605.2 4.0 copy-start.3
  682.4 11.0 %copy-start.1 = (bf16[1024,4,384]{2,1,0:T(4,128)(2,1)S(1)}, bf16[1024,4,384]{2,1,0:T(4,128)(2,1)}, u32[]{:S(2)}) copy-start(bf16[1024,4,384]{2,1,0:T(4,128)(2,1)} %param.11) | copy-start | bytes 9437188
Sparse Core Ops, SparseCore 0:
  78.5 27.4 reduce-scatter.3
  108.6 54.5 reduce-scatter.5
  165.7 34.3 reduce-scatter.7
  605.3 77.0 all-gather.1
where the time goes:
time: 701 us; the launch traced here: 700 us
  waiting for transfers between devices  488 us (70%)
  blocking collectives  58.3 us (8%)
  local copies, waits for them, and re-layouts  54.7 us (8%)
  matrix products  32.5 us (5%)
  starting transfers between devices  24 us (3%)
  other arithmetic  23.2 us (3%)
  between operations  16.3 us (2%)
    ppermute x8, waiting for transfers between devices, partner_2(): lax.ppermute(value, axis, [(i, i ^ 1 << apart) for i in range(lax.axis_si...  290 us
    reduce_scatter x3, waiting for transfers between devices, reduced_to_own(): pieces = lax.psum_scatter(pieces, axes[k], scatter_dimension=0, tiled=True)  122 us
    all_gather x1, waiting for transfers between devices, body(): every_block = lax.all_gather(feature_rows, REPLICA, axis=0, tiled=True)  70.9 us
    psum x4, blocking collectives, one_axis_at_a_time(): return functools.reduce(lax.psum, axes, value)  34.6 us
    ppermute x8, starting transfers between devices, partner_2(): lax.ppermute(value, axis, [(i, i ^ 1 << apart) for i in range(lax.axis_si...  20.4 us
    dot_general x4, matrix products, piece_product(): lax.dot_general(activations, douts, (((0,), (0,)), ((), ())), preferred_e...  19.8 us
    gather x1, local copies, waits for them, and re-layouts, body(): grads_slot = jnp.take(output_grads, source, axis=1)  16.4 us
    dynamic_update_slice x8, local copies, waits for them, and re-layouts, body(): lax.map(piece_product, jnp.arange(rows_dev * lax.axis_size(REPLICA) // pi...  14.5 us
  transfers between devices with their start and end apart: 13, of which 11 were waited for; matrix products, arithmetic and copies ran while one was open for 3% of the time, Pallas kernels for 0%

commit v1 on v0

v1 whole, which is shorter than its diff:
```python
import jax
import jax.numpy as jnp
from jax import lax
from jax.experimental import pallas as pl
from jax.experimental.pallas import tpu as pltpu
from jax.sharding import Mesh
from jax.sharding import PartitionSpec as P

SIZES = {"x": 4, "z": 8, "c": 2, "y": 4}
REPLICA = ("x", "z", "c")
EVERY = ("x", "z", "c", "y")
PLANE = ("z", "c", "y")

beta_stat = 0.9
beta_first = 0.9
beta_second = 0.999
eps_adam = 1e-08
eps_norm = 1e-06


def shifted(value, axis, by):
    n = SIZES[axis]
    return lax.ppermute(value, axis, [(i, (i + by) % n) for i in range(n)])


def outward(n):
    return sorted(range(1, n), key=lambda d: -min(d, n - d))


def window(pieces, start, count, axis):
    return lax.dynamic_slice_in_dim(jnp.concatenate(pieces, axis), start, count, axis)


def gathered(value, axis, dim):
    n = SIZES[axis]
    length = value.shape[dim]
    came = {0: value}
    for d in outward(n):
        came[d] = shifted(value, axis, d)
    ring = [came[(-k) % n] for k in range(n)]
    start = (-lax.axis_index(axis)) % n
    return window(ring + ring[:-1], start * length, n * length, dim)


def scattered_sum(pieces, axis):
    n = SIZES[axis]
    turned = lax.dynamic_slice_in_dim(
        jnp.concatenate([pieces, pieces[:-1]], 0), lax.axis_index(axis), n, 0
    )
    total = turned[0]
    for d in outward(n):
        total = total + shifted(turned[d].astype(jnp.bfloat16), axis, d).astype(jnp.float32)
    return total


def by_core(mine, theirs, core, dim):
    return jnp.where(
        core == 0, jnp.stack([mine, theirs], dim), jnp.stack([theirs, mine], dim)
    )


def place_kernel(distance, core, *refs):
    out = refs[-1]
    mine, theirs = (refs[:4], refs[4:8])
    block = pl.program_id(0)
    for d in range(4):
        for k in range(2):

            @pl.when((distance[block] == d) & (core[0] == k))
            def _():
                out[0, :, k] = mine[d][...]
                out[0, :, 1 - k] = theirs[d][...]


def place_blocks(distance, core, mine, theirs):
    rows, width = mine[0].shape
    part = (8, rows // 8, width)
    whole = pl.BlockSpec(part, lambda b, *_: (0, 0, 0))
    out = pl.pallas_call(
        place_kernel,
        grid_spec=pltpu.PrefetchScalarGridSpec(
            num_scalar_prefetch=2,
            grid=(4,),
            in_specs=[whole] * 8,
            out_specs=pl.BlockSpec((1, 8, 2, *part[1:]), lambda b, *_: (b, 0, 0, 0, 0)),
        ),
        out_shape=jax.ShapeDtypeStruct((4, 8, 2, *part[1:]), jnp.bfloat16),
        compiler_params=pltpu.CompilerParams(vmem_limit_bytes=32 << 20),
        cost_estimate=pl.CostEstimate(flops=0, bytes_accessed=16 * rows * width, transcendentals=0),
        name="place_blocks",
    )(distance, core, *[v.reshape(part) for v in mine + theirs])
    return out.reshape(4, 2 * rows, width)


def root_pairs():
    pairs = []
    for z in range(8):
        for c in range(2):
            for y in range(4):
                line = (z % 2) * 8 + c * 4 + y
                pairs.append(((z * 2 + c) * 4 + y, line * 4 + z // 2))
    return pairs


def body(
    activations,
    output_grads,
    owner,
    step_count,
    statistics,
    inverse_roots,
    first_moment,
    second_moment,
):
    bf, f32 = (jnp.bfloat16, jnp.float32)
    width = activations.shape[1]
    blocks, cols = output_grads.shape[1:]
    span = statistics.shape[0]
    slab = 4 * span
    x, z, core, y = (lax.axis_index(a) for a in EVERY)
    slots = jnp.arange(blocks, dtype=jnp.int32)
    source = jnp.sum((owner[None, :] == slots[:, None]).astype(jnp.int32) * slots[None, :], axis=1)

    right_rows = lax.ppermute(inverse_roots[:, 1, :], PLANE, root_pairs())
    right_root = lax.all_gather(right_rows, ("z", "c"), axis=0, tiled=True)
    left_root = lax.all_gather(inverse_roots[:, 0, :], ("z", "y"), axis=0, tiled=True)

    product = lax.dot_general(
        activations,
        output_grads.reshape(activations.shape[0], blocks * cols),
        (((0,), (0,)), ((), ())),
        preferred_element_type=f32,
    ).reshape(8, 2, slab, blocks * cols)
    total = None
    for d in (2, 1, 3, 0):
        first = lax.dynamic_index_in_dim(source, (x + d) % 4, 0, keepdims=False) * cols

        def half(which):
            return lax.dynamic_slice(product, (0, which, 0, first), (8, 1, slab, cols))[:, 0]

        pair = half(core) + shifted(half(1 - core).astype(bf), "c", 1).astype(f32)
        if d:
            pair = shifted(pair.astype(bf), "x", d).astype(f32)
        total = pair if total is None else total + pair
    reduced = scattered_sum(total, "z")
    slab_rows = gathered(reduced.astype(bf), "y", 1)

    right_part = lax.dot_general(
        slab_rows, right_root, (((1,), (1,)), ((), ())), preferred_element_type=f32
    ).astype(bf)
    right_half = gathered(right_part, "z", 0).reshape(8, slab, cols)
    right_all = by_core(right_half, shifted(right_half, "c", 1), core, 1).reshape(width, cols)
    precond = jnp.dot(left_root, right_all, preferred_element_type=f32)

    rounded = lax.dynamic_slice_in_dim(slab_rows, y * span, span, 0)
    exact = rounded.astype(f32)
    count = step_count[0].astype(f32)
    first_new = beta_first * first_moment + (1.0 - beta_first) * exact
    second_new = beta_second * second_moment + (1.0 - beta_second) * exact * exact
    first_hat = first_new / (1.0 - jnp.power(beta_first, count))
    second_hat = second_new / (1.0 - jnp.power(beta_second, count))
    adam = first_hat / (jnp.sqrt(second_hat) + eps_adam)
    adam_squares = lax.psum(jnp.sum(adam * adam), "z")
    squares = lax.psum(jnp.stack([adam_squares, jnp.sum(precond * precond)]), ("c", "y"))
    scale = jnp.sqrt(squares[0]) / (jnp.sqrt(squares[1]) + eps_norm)
    grafted = (precond * scale).astype(bf)
    mine, theirs = ([grafted] * 4, [shifted(grafted, "c", 1)] * 4)
    for d in (2, 1, 3):
        mine[d] = shifted(grafted, "x", d)
        theirs[d] = shifted(mine[d], "c", 1)
    update = place_blocks((x - owner) % 4, core.reshape(1), mine, theirs)

    half_grad = lax.all_gather(slab_rows, "z", axis=0)
    full_grad = by_core(half_grad, shifted(half_grad, "c", 1), core, 1).reshape(width, width)
    first_column = ((z * 2 + core) * 4 + y) * span
    grad_columns = lax.dynamic_slice_in_dim(full_grad, first_column, span, 1)
    left_gram = lax.dot_general(
        rounded, full_grad, (((1,), (1,)), ((), ())), preferred_element_type=f32
    )
    right_gram = lax.dot_general(
        grad_columns, full_grad, (((0,), (0,)), ((), ())), preferred_element_type=f32
    )
    new_stats = beta_stat * statistics + (1.0 - beta_stat) * jnp.stack([left_gram, right_gram], 1)
    return (new_stats, first_new, second_new, update)


def solution(mesh):
    torus = Mesh(mesh.devices.reshape(*SIZES.values()), EVERY)
    placed = (
        P(REPLICA, None),
        P(REPLICA, None, "y"),
        P(),
        P(),
        P(EVERY, None, None),
        P(EVERY, None, None),
        P(EVERY, None),
        P(EVERY, None),
    )
    return jax.shard_map(
        body,
        mesh=torus,
        in_specs=placed,
        out_specs=(P(EVERY, None, None), P(EVERY, None), P(EVERY, None), P(None, None, "y")),
        check_vma=False,
    )
```

time: 701 us -> 318 us (0.45)
  waiting for transfers between devices: 488 us -> 148 us
  starting transfers between devices: 24 us -> 57.4 us
  blocking collectives: 58.3 us -> 30.9 us
  local copies, waits for them, and re-layouts: 54.7 us -> 27.8 us
  matrix products: 32.5 us -> 18.3 us
  other arithmetic: 23.2 us -> 12.7 us
    ppermute x8 -> x34, waiting for transfers between devices: 290 us -> 75.1 us  [the longest x33 73.7 us: shifted(): return lax.ppermute(value, axis, [(i, (i + by) % n) for i in range(n)])]
    reduce_scatter x3 -> x0, waiting for transfers between devices: 122 us -> none  [reduced_to_own(): pieces = lax.psum_scatter(pieces, axes[k], scatter_dimension=0, tiled=True)]
    ppermute x8 -> x34, starting transfers between devices: 20.4 us -> 57.3 us  [the longest x33 51.3 us: shifted(): return lax.ppermute(value, axis, [(i, (i + by) % n) for i in range(n)])]
    all_to_all x3 -> x0, blocking collectives: 23.7 us -> none  [the longest x1 8.1 us: body(): lax.all_to_all(reduced.astype(jnp.bfloat16), 'shard', split_axis=0, conca...]
    gather x2 -> x0, local copies, waits for them, and re-layouts: 22.3 us -> none  [the longest x1 16.4 us: body(): grads_slot = jnp.take(output_grads, source, axis=1)]
    select_n x11 -> x3, other arithmetic: 17.8 us -> 3.26 us  [the longest x2 3.25 us: by_core(): jnp.where(core == 0, jnp.stack([mine, theirs], dim), jnp.stack([theirs, m...]
    dynamic_update_slice x8 -> x0, local copies, waits for them, and re-layouts: 14.5 us -> none  [body(): lax.map(piece_product, jnp.arange(rows_dev * lax.axis_size(REPLICA) // pi...]
    dot_general x6 -> x3, matrix products: 27.6 us -> 15.3 us  [the longest x1 9.9 us: body(): lax.dot_general(activations, output_grads.reshape(activations.shape[0], b...]
  transfers between devices with their start and end apart: 13 -> 37, of which waited for: 11 -> 20; matrix products, arithmetic and copies ran while one was open for 3% -> 9% of each run, Pallas kernels for 0% -> 1%
where the time goes in v1:
time: 318 us
  waiting for transfers between devices  148 us (47%)
  starting transfers between devices  57.4 us (18%)
  blocking collectives  30.9 us (10%)
  local copies, waits for them, and re-layouts  27.8 us (9%)
  between operations  18.9 us (6%)
  matrix products  18.3 us (6%)
  other arithmetic  12.7 us (4%)
  Pallas kernels  3.3 us (1%)
    ppermute x33, waiting for transfers between devices, shifted(): return lax.ppermute(value, axis, [(i, (i + by) % n) for i in range(n)])  73.7 us
    all_gather x1, waiting for transfers between devices, body(): lax.all_gather(inverse_roots[:, 0, :], ('z', 'y'), axis=0, tiled=True)  58.9 us
    ppermute x33, starting transfers between devices, shifted(): return lax.ppermute(value, axis, [(i, (i + by) % n) for i in range(n)])  51.3 us
    psum x1, blocking collectives, body(): lax.psum(jnp.stack([adam_squares, jnp.sum(precond * precond)]), ('c', 'y'))  17.6 us
    all_gather x1, waiting for transfers between devices, body(): half_grad = lax.all_gather(slab_rows, 'z', axis=0)  14.2 us
    psum x1, blocking collectives, body(): adam_squares = lax.psum(jnp.sum(adam * adam), 'z')  13.2 us
    ppermute x7, local copies, waits for them, and re-layouts, shifted(): return lax.ppermute(value, axis, [(i, (i + by) % n) for i in range(n)])  10.1 us
    dot_general x1, matrix products, body(): lax.dot_general(activations, output_grads.reshape(activations.shape[0], b...  9.9 us
  transfers between devices with their start and end apart: 37, of which 20 were waited for; matrix products, arithmetic and copies ran while one was open for 9% of the time, Pallas kernels for 1%

profile of v1, /device:TPU:1, one launch (start us, length us, event | category | flops | bytes accessed | tf_op | source)
XLA Modules:
  0.0 317.7 jit_solution(12920055003141656327)
XLA Ops:
  11.3 4.8 %copy.45 = bf16[1024,1536]{0,1:T(8,128)(2,1)} copy(bf16[1024,1536]{1,0:T(8,128)(2,1)} %param.8) | data formatting | bytes 6291456 | tf_op args[0]
  16.1 2.7 reshape.105
  18.8 9.9 %fusion = f32[8,2,96,1536]{3,2,1,0:T(8,128)} fusion(bf16[8,2,96,1024]{3,2,1,0:T(8,128)(2,1)} %bitcast.136, bf16[1024,1536,1,1]{1,0,2,3:T(8,128)(2,1)} %reshape.105), kind=kOutput, calls=%fused_computation.1 | convolution fusion | flops 4831838208 | bytes 15728640 | tf_op jit(solution)/shard_map/dot_general | solution.py:128
  28.7 2.6 fusion.11
  31.4 3.3 %collective-permute-start = (bf16[8,96,384]{2,1,0:T(8,128)(2,1)S(1)}, bf16[8,96,384]{2,1,0:T(8,128)(2,1)S(1)}, u32[]{:S(2)}, u32[]{:S(2)}) collective-permute-start(bf16[8,96,384]{2,1,0:T(8,128)(2,1)S(1)} %get-tuple-element.26), channel_id=1, source_target_pairs={{0,4},{4,0},{1,5},{5,1},{2,6},{6,2},{3,7},{7,3},{8,12},{12,8},{9,1... | collective-permute-start | bytes 1769480 | tf_op jit(solution)/shard_map/ppermute | solution.py:23
  39.0 3.7 %fusion.8 = (bf16[8,96,384]{2,1,0:T(8,128)(2,1)}, bf16[8,96,384]{2,1,0:T(8,128)(2,1)}, bf16[8,96,384]{2,1,0:T(8,128)(2,1)}) fusion(bf16[8,96,384]{2,1,0:T(8,128)(2,1)S(1)} %collective-permute-done, f32[8,2,96,1536]{3,2,1,0:T(8,128)} %fusion, s32[]{:T(128)S(6)} %select_n.117, s32[]{:T(128)S(6)} %select_n.120, bf16[8,96,384]{2,1,0:T(8,128)(2,1)} %collective-permute-done.4, ...), kind=kLoop, calls=%fused_computation.21 | loop fusion | flops 2654208 | bytes 7077904 | tf_op jit(solution)/shard_map/convert_element_type | solution.py:143
  45.4 6.0 %collective-permute-start.18 = (bf16[24,1536]{1,0:T(8,128)(2,1)S(1)}, bf16[24,1536]{1,0:T(8,128)(2,1)S(1)}, u32[]{:S(2)}, u32[]{:S(2)}) collective-permute-start(bf16[24,1536]{1,0:T(8,128)(2,1)S(1)} %bitcast.143), channel_id=1, source_target_pairs={{0,0},{1,4},{2,8},{3,12},{4,16},{5,20},{6,24},{7,28},{8,32},{9,36}... | collective-permute-start | bytes 221192 | tf_op jit(solution)/shard_map/ppermute | solution.py:124
  53.5 3.9 %collective-permute-done.5 = bf16[8,96,384]{2,1,0:T(8,128)(2,1)S(1)} collective-permute-done((bf16[8,96,384]{2,1,0:T(8,128)(2,1)}, bf16[8,96,384]{2,1,0:T(8,128)(2,1)S(1)}, u32[]{:S(2)}, u32[]{:S(2)}) %collective-permute-start.5) | collective-permute-done | bytes 589856 | tf_op jit(solution)/shard_map/ppermute | solution.py:23
  57.5 2.6 collective-permute-done.3
  60.0 10.8 %collective-permute-done.1 = bf16[8,96,384]{2,1,0:T(8,128)(2,1)S(1)} collective-permute-done((bf16[8,96,384]{2,1,0:T(8,128)(2,1)}, bf16[8,96,384]{2,1,0:T(8,128)(2,1)S(1)}, u32[]{:S(2)}, u32[]{:S(2)}) %collective-permute-start.1) | collective-permute-done | bytes 589856 | tf_op jit(solution)/shard_map/ppermute | solution.py:23
  72.8 5.6 %collective-permute-start.13 = (bf16[96,384]{1,0:T(8,128)(2,1)S(1)}, bf16[96,384]{1,0:T(8,128)(2,1)S(1)}, u32[]{:S(2)}, u32[]{:S(2)}) collective-permute-start(bf16[96,384]{1,0:T(8,128)(2,1)S(1)} %get-tuple-element.31), channel_id=1, source_target_pairs={{0,56},{8,0},{16,8},{24,16},{32,24},{40,32},{48,40},{56,48},{1,57}... | collective-permute-start | bytes 221192 | tf_op jit(solution)/shard_map/ppermute | solution.py:23
  84.1 3.6 %collective-permute-start.7 = (bf16[96,384]{1,0:T(8,128)(2,1)S(1)}, bf16[96,384]{1,0:T(8,128)(2,1)S(1)}, u32[]{:S(2)}, u32[]{:S(2)}) collective-permute-start(bf16[96,384]{1,0:T(8,128)(2,1)S(1)} %get-tuple-element.30), channel_id=1, source_target_pairs={{0,32},{8,40},{16,48},{24,56},{32,0},{40,8},{48,16},{56,24},{1,33}... | collective-permute-start | bytes 221192 | tf_op jit(solution)/shard_map/ppermute | solution.py:23
  87.7 4.3 %collective-permute-done.8 = bf16[96,384]{1,0:T(8,128)(2,1)S(1)} collective-permute-done((bf16[96,384]{1,0:T(8,128)(2,1)S(1)}, bf16[96,384]{1,0:T(8,128)(2,1)S(1)}, u32[]{:S(2)}, u32[]{:S(2)}) %collective-permute-start.8) | collective-permute-done | bytes 73760 | tf_op jit(solution)/shard_map/ppermute | solution.py:23
  92.0 4.0 %collective-permute-done.7 = bf16[96,384]{1,0:T(8,128)(2,1)S(1)} collective-permute-done((bf16[96,384]{1,0:T(8,128)(2,1)S(1)}, bf16[96,384]{1,0:T(8,128)(2,1)S(1)}, u32[]{:S(2)}, u32[]{:S(2)}) %collective-permute-start.7) | collective-permute-done | bytes 73760 | tf_op jit(solution)/shard_map/ppermute | solution.py:23
  99.9 3.3 %collective-permute-done.15 = bf16[96,384]{1,0:T(8,128)(2,1)S(1)} collective-permute-done((bf16[96,384]{1,0:T(8,128)(2,1)S(1)}, bf16[96,384]{1,0:T(8,128)(2,1)S(1)}, u32[]{:S(2)}, u32[]{:S(2)}) %collective-permute-start.15) | collective-permute-done | bytes 73760 | tf_op jit(solution)/shard_map/ppermute | solution.py:23
  109.4 2.9 collective-permute-start.20
  112.4 4.1 %collective-permute-start.21 = (bf16[96,384]{1,0:T(8,128)(2,1)S(1)}, bf16[96,384]{1,0:T(8,128)(2,1)S(1)}, u32[]{:S(2)}, u32[]{:S(2)}) collective-permute-start(bf16[96,384]{1,0:T(8,128)(2,1)S(1)} %get-tuple-element.46), channel_id=1, source_target_pairs={{0,40},{8,48},{16,56},{24,0},{32,8},{40,16},{48,24},{56,32},{1,41}... | collective-permute-start | bytes 221192 | tf_op jit(solution)/shard_map/ppermute | solution.py:23
  119.6 2.6 collective-permute-start.25
  122.3 4.4 %collective-permute-done.22 = bf16[96,384]{1,0:T(8,128)(2,1)S(1)} collective-permute-done((bf16[96,384]{1,0:T(8,128)(2,1)S(1)}, bf16[96,384]{1,0:T(8,128)(2,1)S(1)}, u32[]{:S(2)}, u32[]{:S(2)}) %collective-permute-start.22) | collective-permute-done | bytes 73760 | tf_op jit(solution)/shard_map/ppermute | solution.py:23
  128.1 3.0 collective-permute-done.24
  131.2 6.9 %collective-permute-done.25 = bf16[96,384]{1,0:T(8,128)(2,1)S(1)} collective-permute-done((bf16[96,384]{1,0:T(8,128)(2,1)S(1)}, bf16[96,384]{1,0:T(8,128)(2,1)S(1)}, u32[]{:S(2)}, u32[]{:S(2)}) %collective-permute-start.25) | collective-permute-done | bytes 73760 | tf_op jit(solution)/shard_map/ppermute | solution.py:23
  138.3 2.4 collective-permute-start.26
  141.5 14.2 %all-gather.8.cloned.1.call-done = bf16[768,1536]{1,0:T(8,128)(2,1)} async-done(((bf16[96,1536]{1,0:T(8,128)(2,1)}), bf16[768,1536]{1,0:T(8,128)(2,1)}) %all-gather.8.cloned.1.call-update) | async-done | bytes 2359312 | tf_op jit(solution)/shard_map/all_gather | solution.py:173
  155.7 3.2 collective-permute-start.17
  160.3 13.2 %psum.14 = f32[1]{0:T(128)} all-reduce(f32[1]{0:T(128)} %bitcast.40), channel_id=1, replica_groups=mesh['x'=4,'z'=8,'c'=2,'y'=4] {'z'}, use_global_device_ids=true, to_apply=%region_2.3 | all-reduce | flops 1 | bytes 8 | tf_op jit(solution)/shard_map/psum | solution.py:163
  173.7 58.9 %all-gather.10.cloned.1.call-done = bf16[768,1,1536]{2,0,1:T(8,128)(2,1)} async-done(((bf16[24,1,1536]{2,0,1:T(8,128)(2,1)}), bf16[768,1,1536]{2,0,1:T(8,128)(2,1)}) %all-gather.10.cloned.1.call-update) | async-done | bytes 2359312 | tf_op jit(solution)/shard_map/all_gather | solution.py:126
  232.7 3.5 %multiply_reduce_fusion = (f32[]{:T(128)}, f32[384,768]{1,0:T(8,128)S(1)}) fusion(bf16[1536,384]{1,0:T(8,128)(2,1)S(1)} %bitcast.141, bf16[768,1,1536]{2,0,1:T(8,128)(2,1)} %all-gather.10.cloned.1.call-done), kind=kOutput, calls=%fused_computation.23 | convolution fusion | flops 906559488 | bytes 4718596 | tf_op jit(solution)/shard_map/dot_general | solution.py:153
  237.6 17.6 %psum.15 = f32[2]{0:T(128)S(1)} all-reduce(f32[2]{0:T(128)S(1)} %pad_maximum_fusion), channel_id=1, replica_groups=mesh['x'=4,'z'=8,'c'=2,'y'=4] {'c','y'}, use_global_device_ids=true, to_apply=%region_4.5 | all-reduce | flops 2 | bytes 16 | tf_op jit(solution)/shard_map/psum | solution.py:164
  262.4 11.3 %collective-permute-done.27 = bf16[768,384]{0,1:T(8,128)(2,1)S(1)} collective-permute-done((bf16[768,384]{0,1:T(8,128)(2,1)S(1)}, bf16[768,384]{0,1:T(8,128)(2,1)S(1)}, u32[]{:S(2)}, u32[]{:S(2)}) %collective-permute-start.27) | collective-permute-done | bytes 589856 | tf_op jit(solution)/shard_map/ppermute | solution.py:23
  274.1 13.3 %collective-permute-done.28 = bf16[768,384]{0,1:T(8,128)(2,1)} collective-permute-done((bf16[768,384]{0,1:T(8,128)(2,1)S(1)}, bf16[768,384]{0,1:T(8,128)(2,1)}, u32[]{:S(2)}, u32[]{:S(2)}) %collective-permute-start.28) | collective-permute-done | bytes 589856 | tf_op jit(solution)/shard_map/ppermute | solution.py:23
  300.5 3.3 %place_blocks.1 = bf16[4,8,2,96,384]{4,3,2,1,0:T(8,128)(2,1)} custom-call(s32[4]{0:T(128)S(1)} %and_select_fusion.distance, s32[1]{0:T(128)} %bitcast.31.core, bf16[8,96,384]{2,1,0:T(8,128)(2,1)S(1)} %bitcast.125, bf16[8,96,384]{2,1,0:T(8,128)(2,1)S(1)} %bitcast.126, bf16[8,96,384]{2,1,0:T(8,128)(2,1)S(1)} %bitcast.127, bf16[8,96,384]{2,1,0:T(8,128)(2,1)S(1)} %bitcast.128, ...), custom_call_target="tpu_custom_call" | custom-call | bytes 4718592 | tf_op jit(solution)/shard_map/place_blocks/pallas_call | solution.py:79
  303.8 3.1 maximum_select_fusion
  (128 shorter events, 59.3 us)
Async XLA Ops:
  7.2 98.5 %all-gather.6.cloned.1.call-start = ((), (), s32[]{:S(2)}) async-start(), calls=%async_computation | async-start | bytes 1253376 | tf_op jit(solution)/shard_map/all_gather | solution.py:125
  31.4 5.0 %collective-permute-start = (bf16[8,96,384]{2,1,0:T(8,128)(2,1)S(1)}, bf16[8,96,384]{2,1,0:T(8,128)(2,1)S(1)}, u32[]{:S(2)}, u32[]{:S(2)}) collective-permute-start(bf16[8,96,384]{2,1,0:T(8,128)(2,1)S(1)} %get-tuple-element.26), channel_id=1, source_target_pairs={{0,4},{4,0},{1,5},{5,1},{2,6},{6,2},{3,7},{7,3},{8,12},{12,8},{9,1... | collective-permute-start | bytes 1769480 | tf_op jit(solution)/shard_map/ppermute | solution.py:23
  35.2 18.3 %collective-permute-start.6 = (bf16[8,96,384]{2,1,0:T(8,128)(2,1)S(1)}, bf16[8,96,384]{2,1,0:T(8,128)(2,1)S(1)}, u32[]{:S(2)}, u32[]{:S(2)}) collective-permute-start(bf16[8,96,384]{2,1,0:T(8,128)(2,1)S(1)} %get-tuple-element.28), channel_id=1, source_target_pairs={{0,4},{4,0},{1,5},{5,1},{2,6},{6,2},{3,7},{7,3},{8,12},{12,8},{9,1... | collective-permute-start | bytes 1769480 | tf_op jit(solution)/shard_map/ppermute | solution.py:23
  42.7 14.8 %collective-permute-start.5 = (bf16[8,96,384]{2,1,0:T(8,128)(2,1)}, bf16[8,96,384]{2,1,0:T(8,128)(2,1)S(1)}, u32[]{:S(2)}, u32[]{:S(2)}) collective-permute-start(bf16[8,96,384]{2,1,0:T(8,128)(2,1)} %get-tuple-element.24), channel_id=1, source_target_pairs={{0,192},{64,0},{128,64},{192,128},{1,193},{65,1},{129,65},{193,129... | collective-permute-start | bytes 1769480 | tf_op jit(solution)/shard_map/ppermute | solution.py:23
  43.5 16.6 %collective-permute-start.3 = (bf16[8,96,384]{2,1,0:T(8,128)(2,1)}, bf16[8,96,384]{2,1,0:T(8,128)(2,1)S(1)}, u32[]{:S(2)}, u32[]{:S(2)}) collective-permute-start(bf16[8,96,384]{2,1,0:T(8,128)(2,1)} %get-tuple-element.25), channel_id=1, source_target_pairs={{0,64},{64,128},{128,192},{192,0},{1,65},{65,129},{129,193},{193,1... | collective-permute-start | bytes 1769480 | tf_op jit(solution)/shard_map/ppermute | solution.py:23
  44.2 26.7 %collective-permute-start.1 = (bf16[8,96,384]{2,1,0:T(8,128)(2,1)}, bf16[8,96,384]{2,1,0:T(8,128)(2,1)S(1)}, u32[]{:S(2)}, u32[]{:S(2)}) collective-permute-start(bf16[8,96,384]{2,1,0:T(8,128)(2,1)} %get-tuple-element.23), channel_id=1, source_target_pairs={{0,128},{64,192},{128,0},{192,64},{1,129},{65,193},{129,1},{193,65... | collective-permute-start | bytes 1769480 | tf_op jit(solution)/shard_map/ppermute | solution.py:23
  45.4 7.4 %collective-permute-start.18 = (bf16[24,1536]{1,0:T(8,128)(2,1)S(1)}, bf16[24,1536]{1,0:T(8,128)(2,1)S(1)}, u32[]{:S(2)}, u32[]{:S(2)}) collective-permute-start(bf16[24,1536]{1,0:T(8,128)(2,1)S(1)} %bitcast.143), channel_id=1, source_target_pairs={{0,0},{1,4},{2,8},{3,12},{4,16},{5,20},{6,24},{7,28},{8,32},{9,36}... | collective-permute-start | bytes 221192 | tf_op jit(solution)/shard_map/ppermute | solution.py:124
  53.5 102.2 %all-gather.8.cloned.1.call-start = ((), (), s32[]{:S(2)}) async-start(), calls=%async_computation.1 | async-start | bytes 2654208 | tf_op jit(solution)/shard_map/all_gather | solution.py:173
  72.8 10.4 %collective-permute-start.13 = (bf16[96,384]{1,0:T(8,128)(2,1)S(1)}, bf16[96,384]{1,0:T(8,128)(2,1)S(1)}, u32[]{:S(2)}, u32[]{:S(2)}) collective-permute-start(bf16[96,384]{1,0:T(8,128)(2,1)S(1)} %get-tuple-element.31), channel_id=1, source_target_pairs={{0,56},{8,0},{16,8},{24,16},{32,24},{40,32},{48,40},{56,48},{1,57}... | collective-permute-start | bytes 221192 | tf_op jit(solution)/shard_map/ppermute | solution.py:23
  78.5 5.6 %collective-permute-start.12 = (bf16[96,384]{1,0:T(8,128)(2,1)S(1)}, bf16[96,384]{1,0:T(8,128)(2,1)S(1)}, u32[]{:S(2)}, u32[]{:S(2)}) collective-permute-start(bf16[96,384]{1,0:T(8,128)(2,1)S(1)} %get-tuple-element.32), channel_id=1, source_target_pairs={{0,8},{8,16},{16,24},{24,32},{32,40},{40,48},{48,56},{56,0},{1,9},... | collective-permute-start | bytes 221192 | tf_op jit(solution)/shard_map/ppermute | solution.py:23
  78.5 9.2 %collective-permute-start.11 = (bf16[96,384]{1,0:T(8,128)(2,1)S(1)}, bf16[96,384]{1,0:T(8,128)(2,1)S(1)}, u32[]{:S(2)}, u32[]{:S(2)}) collective-permute-start(bf16[96,384]{1,0:T(8,128)(2,1)S(1)} %get-tuple-element.33), channel_id=1, source_target_pairs={{0,48},{8,56},{16,0},{24,8},{32,16},{40,24},{48,32},{56,40},{1,49}... | collective-permute-start | bytes 221192 | tf_op jit(solution)/shard_map/ppermute | solution.py:23
  80.4 7.3 %collective-permute-start.10 = (bf16[96,384]{1,0:T(8,128)(2,1)S(1)}, bf16[96,384]{1,0:T(8,128)(2,1)S(1)}, u32[]{:S(2)}, u32[]{:S(2)}) collective-permute-start(bf16[96,384]{1,0:T(8,128)(2,1)S(1)} %get-tuple-element.34), channel_id=1, source_target_pairs={{0,16},{8,24},{16,32},{24,40},{32,48},{40,56},{48,0},{56,8},{1,17}... | collective-permute-start | bytes 221192 | tf_op jit(solution)/shard_map/ppermute | solution.py:23
  80.9 6.9 %collective-permute-start.9 = (bf16[96,384]{1,0:T(8,128)(2,1)S(1)}, bf16[96,384]{1,0:T(8,128)(2,1)S(1)}, u32[]{:S(2)}, u32[]{:S(2)}) collective-permute-start(bf16[96,384]{1,0:T(8,128)(2,1)S(1)} %get-tuple-element.35), channel_id=1, source_target_pairs={{0,40},{8,48},{16,56},{24,0},{32,8},{40,16},{48,24},{56,32},{1,41}... | collective-permute-start | bytes 221192 | tf_op jit(solution)/shard_map/ppermute | solution.py:23
  83.3 8.8 %collective-permute-start.8 = (bf16[96,384]{1,0:T(8,128)(2,1)S(1)}, bf16[96,384]{1,0:T(8,128)(2,1)S(1)}, u32[]{:S(2)}, u32[]{:S(2)}) collective-permute-start(bf16[96,384]{1,0:T(8,128)(2,1)S(1)} %get-tuple-element.36), channel_id=1, source_target_pairs={{0,24},{8,32},{16,40},{24,48},{32,56},{40,0},{48,8},{56,16},{1,25}... | collective-permute-start | bytes 221192 | tf_op jit(solution)/shard_map/ppermute | solution.py:23
  84.1 11.9 %collective-permute-start.7 = (bf16[96,384]{1,0:T(8,128)(2,1)S(1)}, bf16[96,384]{1,0:T(8,128)(2,1)S(1)}, u32[]{:S(2)}, u32[]{:S(2)}) collective-permute-start(bf16[96,384]{1,0:T(8,128)(2,1)S(1)} %get-tuple-element.30), channel_id=1, source_target_pairs={{0,32},{8,40},{16,48},{24,56},{32,0},{40,8},{48,16},{56,24},{1,33}... | collective-permute-start | bytes 221192 | tf_op jit(solution)/shard_map/ppermute | solution.py:23
  104.9 127.8 %all-gather.10.cloned.1.call-start = ((), (), s32[]{:S(2)}) async-start(), calls=%async_computation.2 | async-start | bytes 2433024 | tf_op jit(solution)/shard_map/all_gather | solution.py:126
  107.5 12.1 %collective-permute-start.19 = (bf16[96,384]{1,0:T(8,128)(2,1)S(1)}, bf16[96,384]{1,0:T(8,128)(2,1)S(1)}, u32[]{:S(2)}, u32[]{:S(2)}) collective-permute-start(bf16[96,384]{1,0:T(8,128)(2,1)S(1)} %get-tuple-element.46), channel_id=1, source_target_pairs={{0,56},{8,0},{16,8},{24,16},{32,24},{40,32},{48,40},{56,48},{1,57}... | collective-permute-start | bytes 221192 | tf_op jit(solution)/shard_map/ppermute | solution.py:23
  109.4 10.2 %collective-permute-start.20 = (bf16[96,384]{1,0:T(8,128)(2,1)S(1)}, bf16[96,384]{1,0:T(8,128)(2,1)S(1)}, u32[]{:S(2)}, u32[]{:S(2)}) collective-permute-start(bf16[96,384]{1,0:T(8,128)(2,1)S(1)} %get-tuple-element.46), channel_id=1, source_target_pairs={{0,48},{8,56},{16,0},{24,8},{32,16},{40,24},{48,32},{56,40},{1,49}... | collective-permute-start | bytes 221192 | tf_op jit(solution)/shard_map/ppermute | solution.py:23
  112.4 9.9 %collective-permute-start.21 = (bf16[96,384]{1,0:T(8,128)(2,1)S(1)}, bf16[96,384]{1,0:T(8,128)(2,1)S(1)}, u32[]{:S(2)}, u32[]{:S(2)}) collective-permute-start(bf16[96,384]{1,0:T(8,128)(2,1)S(1)} %get-tuple-element.46), channel_id=1, source_target_pairs={{0,40},{8,48},{16,56},{24,0},{32,8},{40,16},{48,24},{56,32},{1,41}... | collective-permute-start | bytes 221192 | tf_op jit(solution)/shard_map/ppermute | solution.py:23
  116.5 10.2 %collective-permute-start.22 = (bf16[96,384]{1,0:T(8,128)(2,1)S(1)}, bf16[96,384]{1,0:T(8,128)(2,1)S(1)}, u32[]{:S(2)}, u32[]{:S(2)}) collective-permute-start(bf16[96,384]{1,0:T(8,128)(2,1)S(1)} %get-tuple-element.46), channel_id=1, source_target_pairs={{0,32},{8,40},{16,48},{24,56},{32,0},{40,8},{48,16},{56,24},{1,33}... | collective-permute-start | bytes 221192 | tf_op jit(solution)/shard_map/ppermute | solution.py:23
  117.9 10.2 %collective-permute-start.23 = (bf16[96,384]{1,0:T(8,128)(2,1)S(1)}, bf16[96,384]{1,0:T(8,128)(2,1)S(1)}, u32[]{:S(2)}, u32[]{:S(2)}) collective-permute-start(bf16[96,384]{1,0:T(8,128)(2,1)S(1)} %get-tuple-element.46), channel_id=1, source_target_pairs={{0,24},{8,32},{16,40},{24,48},{32,56},{40,0},{48,8},{56,16},{1,25}... | collective-permute-start | bytes 221192 | tf_op jit(solution)/shard_map/ppermute | solution.py:23
  119.6 11.5 %collective-permute-start.24 = (bf16[96,384]{1,0:T(8,128)(2,1)S(1)}, bf16[96,384]{1,0:T(8,128)(2,1)S(1)}, u32[]{:S(2)}, u32[]{:S(2)}) collective-permute-start(bf16[96,384]{1,0:T(8,128)(2,1)S(1)} %get-tuple-element.46), channel_id=1, source_target_pairs={{0,16},{8,24},{16,32},{24,40},{32,48},{40,56},{48,0},{56,8},{1,17}... | collective-permute-start | bytes 221192 | tf_op jit(solution)/shard_map/ppermute | solution.py:23
  119.6 18.4 %collective-permute-start.25 = (bf16[96,384]{1,0:T(8,128)(2,1)S(1)}, bf16[96,384]{1,0:T(8,128)(2,1)S(1)}, u32[]{:S(2)}, u32[]{:S(2)}) collective-permute-start(bf16[96,384]{1,0:T(8,128)(2,1)S(1)} %get-tuple-element.46), channel_id=1, source_target_pairs={{0,8},{8,16},{16,24},{24,32},{32,40},{40,48},{48,56},{56,0},{1,9},... | collective-permute-start | bytes 221192 | tf_op jit(solution)/shard_map/ppermute | solution.py:23
  138.3 35.3 %collective-permute-start.26 = (bf16[8,96,384]{2,1,0:T(8,128)(2,1)S(1)}, bf16[8,96,384]{2,1,0:T(8,128)(2,1)S(1)}, u32[]{:S(2)}, u32[]{:S(2)}) collective-permute-start(bf16[8,96,384]{2,1,0:T(8,128)(2,1)S(1)} %bitcast.137), channel_id=1, source_target_pairs={{0,4},{4,0},{1,5},{5,1},{2,6},{6,2},{3,7},{7,3},{8,12},{12,8},{9,1... | collective-permute-start | bytes 1769480 | tf_op jit(solution)/shard_map/ppermute | solution.py:23
  155.7 148.1 %collective-permute-start.17 = (bf16[8,96,1536]{2,1,0:T(8,128)(2,1)}, bf16[8,96,1536]{2,1,0:T(8,128)(2,1)}, u32[]{:S(2)}, u32[]{:S(2)}) collective-permute-start(bf16[8,96,1536]{2,1,0:T(8,128)(2,1)} %bitcast.139), channel_id=1, source_target_pairs={{0,4},{4,0},{1,5},{5,1},{2,6},{6,2},{3,7},{7,3},{8,12},{12,8},{9,1... | collective-permute-start | bytes 7077896 | tf_op jit(solution)/shard_map/ppermute | solution.py:23
  257.3 16.5 %collective-permute-start.27 = (bf16[768,384]{0,1:T(8,128)(2,1)S(1)}, bf16[768,384]{0,1:T(8,128)(2,1)S(1)}, u32[]{:S(2)}, u32[]{:S(2)}) collective-permute-start(bf16[768,384]{0,1:T(8,128)(2,1)S(1)} %fusion.10), channel_id=1, source_target_pairs={{0,64},{64,128},{128,192},{192,0},{1,65},{65,129},{129,193},{193,1... | collective-permute-start | bytes 1769480 | tf_op jit(solution)/shard_map/ppermute | solution.py:23
  258.5 28.9 %collective-permute-start.28 = (bf16[768,384]{0,1:T(8,128)(2,1)S(1)}, bf16[768,384]{0,1:T(8,128)(2,1)}, u32[]{:S(2)}, u32[]{:S(2)}) collective-permute-start(bf16[768,384]{0,1:T(8,128)(2,1)S(1)} %fusion.10), channel_id=1, source_target_pairs={{0,128},{64,192},{128,0},{192,64},{1,129},{65,193},{129,1},{193,65... | collective-permute-start | bytes 1769480 | tf_op jit(solution)/shard_map/ppermute | solution.py:23
  260.9 26.9 %collective-permute-start.29 = (bf16[768,384]{0,1:T(8,128)(2,1)S(1)}, bf16[768,384]{0,1:T(8,128)(2,1)}, u32[]{:S(2)}, u32[]{:S(2)}) collective-permute-start(bf16[768,384]{0,1:T(8,128)(2,1)S(1)} %fusion.10), channel_id=1, source_target_pairs={{0,192},{64,0},{128,64},{192,128},{1,193},{65,1},{129,65},{193,129... | collective-permute-start | bytes 1769480 | tf_op jit(solution)/shard_map/ppermute | solution.py:23
  262.1 29.2 %collective-permute-start.30 = (bf16[768,384]{0,1:T(8,128)(2,1)S(1)}, bf16[768,384]{0,1:T(8,128)(2,1)}, u32[]{:S(2)}, u32[]{:S(2)}) collective-permute-start(bf16[768,384]{0,1:T(8,128)(2,1)S(1)} %fusion.10), channel_id=1, source_target_pairs={{0,4},{4,0},{1,5},{5,1},{2,6},{6,2},{3,7},{7,3},{8,12},{12,8},{9,1... | collective-permute-start | bytes 1769480 | tf_op jit(solution)/shard_map/ppermute | solution.py:23
  273.7 18.9 %collective-permute-start.31 = (bf16[768,384]{0,1:T(8,128)(2,1)S(1)}, bf16[768,384]{0,1:T(8,128)(2,1)}, u32[]{:S(2)}, u32[]{:S(2)}) collective-permute-start(bf16[768,384]{0,1:T(8,128)(2,1)S(1)} %collective-permute-done.27), channel_id=1, source_target_pairs={{0,4},{4,0},{1,5},{5,1},{2,6},{6,2},{3,7},{7,3},{8,12},{12,8},{9,1... | collective-permute-start | bytes 1769480 | tf_op jit(solution)/shard_map/ppermute | solution.py:23
  287.4 6.7 %collective-permute-start.32 = (bf16[768,384]{0,1:T(8,128)(2,1)}, bf16[768,384]{0,1:T(8,128)(2,1)}, u32[]{:S(2)}, u32[]{:S(2)}) collective-permute-start(bf16[768,384]{0,1:T(8,128)(2,1)} %collective-permute-done.28), channel_id=1, source_target_pairs={{0,4},{4,0},{1,5},{5,1},{2,6},{6,2},{3,7},{7,3},{8,12},{12,8},{9,1... | collective-permute-start | bytes 1769480 | tf_op jit(solution)/shard_map/ppermute | solution.py:23
  287.8 8.4 %collective-permute-start.33 = (bf16[768,384]{0,1:T(8,128)(2,1)}, bf16[768,384]{0,1:T(8,128)(2,1)}, u32[]{:S(2)}, u32[]{:S(2)}) collective-permute-start(bf16[768,384]{0,1:T(8,128)(2,1)} %collective-permute-done.29), channel_id=1, source_target_pairs={{0,4},{4,0},{1,5},{5,1},{2,6},{6,2},{3,7},{7,3},{8,12},{12,8},{9,1... | collective-permute-start | bytes 1769480 | tf_op jit(solution)/shard_map/ppermute | solution.py:23
  (16 other events, 204.8 us)
Sparse Core Ops, SparseCore 0:
  53.6 47.8 all-gather.5
  105.0 50.6 all-gather.7
  158.8 73.7 all-gather.9
